TPU v7x, 128 devices: a whole 4x4x4 slice. The times are simulated.
128 devices in a mesh: img: 8 (over x, core), pos: 16 (over z, y).
Axes of the slice: x: 4, y: 4, z: 4, core: 2. Of those that a mesh axis runs over, the one named last changes fastest.
Arguments:
- features: bfloat16 [16384, 32, 1536], P(('img', 'pos')), may hold values from -6 to 6
- channel_index: int32 [550], replicated, may hold values from 0 to 1535, as said below
- image_counts: int32 [128], P(('img', 'pos')), may hold values from 32 to 128, as said below
Outputs:
- centres: float32 [32, 550], P('pos')
- covars: float32 [32, 550, 550], P('pos')
Inputs may be any that keep to these rules, and one draw needn't show every extreme that they name: `channel_index`: distinct channel numbers. `image_counts`: some device uses all 128 slots and some only a quarter.
All inputs are finite; a program needn't handle non-finite values.
Results may differ from a plain program's by a relative error of at most 0.0003.
Values may be sent and summed in bfloat16 or wider, within the bound.
A program may use at most 128 MiB of HBM per device.

v0:
```python
import jax
import jax.numpy as jnp
from jax import lax
from jax.sharding import PartitionSpec as P

REG = 0.01


def combined_all(value, axis, combine):
    everything = jax.tree.map(lambda part: lax.all_gather(part, axis), value)
    initial = jax.tree.map(lambda part: part[0], everything)

    def lap(k, so_far):
        return combine(so_far, jax.tree.map(lambda part: part[k], everything))

    return lax.fori_loop(1, lax.axis_size(axis), lap, initial)


def moments(received):
    rows = received[:, 0]
    sq_sum = jnp.einsum("ipk,ipl->pkl", rows, rows, preferred_element_type=jnp.float32)
    lin_sum = jnp.sum(rows.astype(jnp.float32), axis=0)
    return (sq_sum, lin_sum)


def body(features, channel_index, image_counts):
    slots = features.shape[0]
    owners = lax.axis_size("pos")
    owned = features.shape[1] // owners
    usable = lax.iota(jnp.int32, slots) < image_counts[0]
    masked = features * usable.astype(jnp.bfloat16)[:, None, None]
    chosen = jnp.take(masked, channel_index, axis=2)
    chosen = chosen.reshape(slots, owners, owned, chosen.shape[2])
    sq_sum, lin_sum = moments(
        lax.all_to_all(chosen, "pos", split_axis=1, concat_axis=0, tiled=True)
    )
    group_total = lax.psum(image_counts.astype(jnp.float32)[0], "pos")
    width = channel_index.shape[0]
    identity_mat = jnp.eye(width, dtype=jnp.float32)
    centre = lin_sum / group_total
    scatter_mat = sq_sum - group_total * centre[:, :, None] * centre[:, None, :]

    def combine(earlier, later):
        count_low, centre_low, scatter_low = earlier
        count_high, centre_high, scatter_high = later
        joined = count_low + count_high
        offset = centre_high - centre_low
        new_centre = centre_low + offset * (count_high / joined)
        weight_pair = count_low * count_high / joined
        new_scatter = (
            scatter_low + scatter_high + weight_pair * offset[:, :, None] * offset[:, None, :]
        )
        return (joined, new_centre, new_scatter)

    total_count, centre, scatter_mat = combined_all(
        (group_total, centre, scatter_mat), "img", combine
    )
    covar = scatter_mat / (total_count - 1.0) + REG * identity_mat
    return (centre, covar)


def solution(mesh):
    placed = (P(("img", "pos"), None, None), P(), P(("img", "pos")))
    return jax.shard_map(
        body,
        mesh=mesh,
        in_specs=placed,
        out_specs=(P("pos", None), P("pos", None, None)),
        check_vma=False,
    )
```

profile of v0, /device:TPU:1, one launch (start us, length us, event | category | flops | bytes accessed | tf_op | source)
XLA Modules:
  0.0 346.5 jit_solution(6363015843126375706)
XLA Ops:
  7.2 0.7 compare_select_fusion
  7.9 0.7 compare_and_fusion
  9.2 17.9 %copy.24 = bf16[128,32,1536]{0,1,2:T(8,128)(2,1)} copy(bf16[128,32,1536]{2,1,0:T(8,128)(2,1)} %param.5) | data formatting | bytes 25165824 | tf_op args[0]
  27.2 10.4 %broadcast_multiply_fusion.1 = bf16[128,32,1536]{0,1,2:T(8,128)(2,1)} fusion(bf16[128,32,1536]{0,1,2:T(8,128)(2,1)} %copy.24, bf16[128]{0:T(256)(128)(2,1)S(1)} %compare_convert_fusion), kind=kLoop, calls=%fused_computation.7 | loop fusion | flops 6291456 | bytes 25166080 | tf_op jit(solution)/shard_map/mul | solution.py:31
  37.6 8.9 %gather_fusion = bf16[550,128,32]{1,2,0:T(8,128)(2,1)} fusion(bf16[128,32,1536]{0,1,2:T(8,128)(2,1)} %broadcast_multiply_fusion.1, s32[1024]{0:T(1024)S(1)} %pad_clamp_fusion), kind=kCustom, calls=%fused_computation | custom fusion | bytes 9013400 | tf_op jit(solution)/shard_map/jit(_take)/gather | solution.py:32
  46.5 4.0 %copy.25 = bf16[128,32,550]{0,2,1:T(8,128)(2,1)S(1)} copy(bf16[128,32,550]{0,1,2:T(8,128)(2,1)} %bitcast.35) | data formatting | bytes 9011200 | tf_op jit(solution)/shard_map/jit(_take)/gather | solution.py:32
  50.5 2.5 broadcast_select_fusion
  53.0 7.9 %copy.26 = bf16[128,16,2,550]{0,2,3,1:T(2,128)(2,1)} copy(bf16[128,16,2,550]{0,3,2,1:T(8,128)(2,1)} %broadcast_select_fusion) | data formatting | bytes 9011200 | tf_op jit(solution)/shard_map/jit(_take)/select_n | solution.py:32
  60.9 8.6 %all-to-all-start = ((bf16[128,16,2,550]{0,2,3,1:T(2,128)(2,1)}), bf16[128,16,2,550]{0,2,3,1:T(2,128)(2,1)}, u32[]{:S(2)}, u32[]{:S(2)}) async-start(bf16[128,16,2,550]{0,2,3,1:T(2,128)(2,1)} %copy.26), calls=%async_computation | async-start | bytes 9011200 | tf_op jit(solution)/shard_map/all_to_all | solution.py:35
  69.6 89.4 %psum.7 = f32[]{:T(128)} all-reduce(f32[]{:T(128)} %bitcast.3), channel_id=1, replica_groups=mesh['img'=8,'pos'=16] {'pos'}, use_global_device_ids=true, to_apply=%region_0.1 | all-reduce | flops 1 | bytes 8 | tf_op jit(solution)/shard_map/psum | solution.py:37
  159.0 5.9 %convert_reduce_fusion = f32[2,550]{0,1:T(8,128)S(1)} fusion(bf16[128,16,2,550]{0,2,3,1:T(2,128)(2,1)} %all-to-all-done), kind=kLoop, calls=%fused_computation.6 | loop fusion | flops 4504500 | bytes 4510000 | tf_op jit(solution)/shard_map/reduce_sum | solution.py:22
  165.0 5.0 %copy.28 = bf16[16,128,1,2,550]{1,0,4,3,2:T(8,128)(2,1)} copy(bf16[16,128,1,2,550]{1,3,4,0,2:T(2,128)(2,1)} %bitcast.11) | data formatting | bytes 9011200 | tf_op jit(solution)/shard_map/all_to_all | solution.py:35
  170.0 5.0 %squeeze.52 = bf16[2048,2,550]{0,2,1:T(8,128)(2,1)} reshape(bf16[16,128,1,2,550]{1,0,4,3,2:T(8,128)(2,1)} %copy.28) | data formatting | bytes 9011200 | tf_op jit(solution)/shard_map/squeeze | solution.py:20
  175.0 0.7 broadcast_multiply_fusion.2
  175.6 8.9 %multiply_subtract_fusion = f32[2,550,550]{2,1,0:T(8,128)} fusion(bf16[2048,2,550]{0,2,1:T(8,128)(2,1)} %squeeze.52, f32[2,550]{1,0:T(2,128)S(1)} %get-tuple-element.200, f32[2,550]{1,0:T(2,128)S(1)} %get-tuple-element.199), kind=kOutput, calls=%fused_computation.9 | convolution fusion | flops 2479289856 | bytes 6934400 | tf_op jit(solution)/shard_map/ipk,ipl->pkl/dot_general | solution.py:21
  184.6 0.6 copy-done.1
  185.2 0.6 dynamic-slice
  185.8 1.4 dynamic-update-slice
  187.2 19.4 %all-reduce = f32[8]{0:T(128)S(1)} all-reduce(f32[8]{0:T(128)S(1)} %dynamic-update-slice), channel_id=1, replica_groups=mesh['img'=8,'pos'=16] {'img'}, use_global_device_ids=true, to_apply=%add | all-reduce | flops 8 | bytes 64
  206.6 1.3 fusion.2
  207.9 13.3 %all-gather.2 = f32[8,2,550]{2,1,0:T(2,128)S(1)} all-gather(f32[1,2,550]{2,1,0:T(2,128)S(1)} %bitcast.38), channel_id=2, replica_groups=mesh['img'=8,'pos'=16] {'img'}, dimensions={0}, use_global_device_ids=true | all-gather | bytes 39600 | tf_op jit(solution)/shard_map/all_gather | solution.py:10
  221.2 76.9 %all-gather.5.cloned.1.call-done = f32[16,550,550]{2,1,0:T(8,128)} async-done(((f32[2,550,550]{2,1,0:T(8,128)}), f32[16,550,550]{2,1,0:T(8,128)}) %all-gather.5.cloned.1.call-update) | async-done | bytes 19360016 | tf_op jit(solution)/shard_map/all_gather | solution.py:10
  298.1 2.0 slice.18
  300.0 33.8 %while.19 = (s32[]{:T(128)}, f32[]{:T(128)}, f32[2,550]{1,0:T(2,128)S(1)}, f32[2,550,550]{2,1,0:T(8,128)S(1)}, f32[8]{0:T(128)S(1)}, /*index=5*/f32[8,2,550]{2,1...) while((s32[]{:T(128)}, f32[]{:T(128)}, f32[2,550]{1,0:T(2,128)S(1)}, ...), condition=%wide.region_3.4_spmd, body=%wide.region_2.3_spmd.sunk | while | flops 1819409 | bytes 7299827 | solution.py:16
  302.4 2.5 fusion.6
  307.2 2.5 fusion.6
  312.1 2.5 fusion.6
  316.9 2.5 fusion.6
  321.7 2.5 fusion.6
  326.5 2.5 fusion.6
  331.4 2.5 fusion.6
  333.9 5.8 %fusion.1 = f32[2,550,550]{2,0,1:T(2,128)} fusion(f32[2,550,550]{2,1,0:T(8,128)S(1)} %get-tuple-element.181, f32[550,550]{1,0:T(8,128)} %fusion.2, f32[]{:T(128)S(6)} %sub.17), kind=kLoop, calls=%fused_computation.11 | loop fusion | flops 1210000 | bytes 6050004 | tf_op jit(solution)/shard_map/add | solution.py:58
  (32 shorter events, 4.4 us)
Async XLA Ops:
  60.9 98.1 %all-to-all-start = ((bf16[128,16,2,550]{0,2,3,1:T(2,128)(2,1)}), bf16[128,16,2,550]{0,2,3,1:T(2,128)(2,1)}, u32[]{:S(2)}, u32[]{:S(2)}) async-start(bf16[128,16,2,550]{0,2,3,1:T(2,128)(2,1)} %copy.26), calls=%async_computation | async-start | bytes 9011200 | tf_op jit(solution)/shard_map/all_to_all | solution.py:35
  69.6 228.5 %all-gather.5.cloned.1.call-start = ((), (), s32[]{:S(2)}) async-start(), calls=%async_computation.1 | async-start | bytes 25436160 | tf_op jit(solution)/shard_map/all_gather | solution.py:10
  184.6 0.7 copy-start.1
  333.8 5.8 %copy-start = (f32[2,550]{1,0:T(2,128)}, f32[2,550]{1,0:T(2,128)S(1)}, u32[]{:S(2)}) copy-start(f32[2,550]{1,0:T(2,128)S(1)} %get-tuple-element.178) | copy-start | bytes 13204
Sparse Core Ops, SparseCore 0:
  184.7 113.2 all-gather.4
where the time goes:
time: 348 us; the launch traced here: 346 us
  blocking collectives  122 us (35%)
  waiting for transfers between devices  76.9 us (22%)
  local copies, waits for them, and re-layouts  57.5 us (17%)
  other arithmetic  45.2 us (13%)
  between operations  14.8 us (4%)
  loops' own time  12.4 us (4%)
  matrix products  8.93 us (3%)
  starting transfers between devices  8.68 us (2%)
    psum x1, blocking collectives, body(): group_total = lax.psum(image_counts.astype(jnp.float32)[0], 'pos')  89.4 us
    all_gather x1, waiting for transfers between devices, combined_all(): everything = jax.tree.map(lambda part: lax.all_gather(part, axis), value)  76.9 us
    unnamed x8, local copies, waits for them, and re-layouts  20.6 us
    unnamed x1, blocking collectives  19.4 us
    add x7, other arithmetic, combine(): scatter_low + scatter_high  17.2 us
    all_gather x1, blocking collectives, combined_all(): everything = jax.tree.map(lambda part: lax.all_gather(part, axis), value)  13.3 us
    gather x2, local copies, waits for them, and re-layouts, body(): chosen = jnp.take(masked, channel_index, axis=2)  13 us
    another operation x1, loops' own time, combined_all(): return lax.fori_loop(1, lax.axis_size(axis), lap, initial)  12.4 us
  transfers between devices with their start and end apart: 2, of which 1 were waited for; matrix products, arithmetic and copies ran while one was open for 1% of the time, Pallas kernels for 0%

commit v1 on v0

v1 whole, which is shorter than its diff:
```python
import functools

import jax
import jax.numpy as jnp
from jax import lax
from jax.experimental import pallas as pl
from jax.experimental.pallas import tpu as pltpu
from jax.sharding import PartitionSpec as P

REG = 0.01
MESH = pl.DeviceIdType.MESH
RING = 4
LANE = 128
F32 = jnp.float32
BF16 = jnp.bfloat16


def sizes(width):
    rows = -(-(width + 1) // 16) * 16
    full = rows // LANE
    strip = rows - full * LANE
    packed = full * (full + 1) // 2 * LANE + strip * (full + 1)
    return rows, full, strip, -(-packed // 32) * 32


def block_row(i, full, strip):
    return i * (i + 1) // 2 * LANE, (LANE if i < full else strip)


def gather_kernel(
    width, feat, chan, count, out,
    slab, onehot, picked, send, recv, part, rs_recv, ar_recv, tot,
    load_sem, send_sem, recv_sem, rs_send, rs_sem, ar_send, ar_sem, ag_send, ag_sem, fw_send, fw_sem, out_sem,
):
    rows, full, strip, packed = sizes(width)
    piece = packed // RING
    images, owned = feat.shape[0], feat.shape[1] // RING
    c_in, cols = onehot.shape
    img, pos = lax.axis_index("img"), lax.axis_index("pos")
    x, c = img // 2, img % 2
    z, y = pos // RING, pos % RING
    ring_b = (1 - c) * y + c * z

    barrier = pltpu.get_barrier_semaphore()

    def greet(i, p):
        pl.semaphore_signal(barrier, inc=1, device_id={"img": i, "pos": p}, device_id_type=MESH)

    for d in range(1, RING):
        for k in range(2):
            greet(2 * x + k, (z + d) % RING * RING + y)
            greet(2 * x + k, z * RING + (y + d) % RING)
        greet((x + d) % RING * 2 + c, pos)
    greet(2 * x + 1 - c, pos)

    def load(t):
        zp = (z + 1 + t) % RING
        return pltpu.make_async_copy(
            feat.at[:, pl.ds(zp * owned, owned), :], slab.at[t], load_sem.at[t]
        )

    for t in range(RING):
        load(t).start()

    tail = width // LANE * LANE
    onehot[:, tail:] = jnp.zeros((c_in, cols - tail), BF16)
    step = 256

    def build(i, carry):
        at = pl.ds(pl.multiple_of(i * step, step), step)
        which = lax.broadcasted_iota(jnp.int32, (step, width), 0) + i * step
        onehot[at, :width] = jnp.where(which == chan[...], 1.0, 0.0).astype(BF16)
        return carry

    lax.fori_loop(0, c_in // step, build, 0)
    last = full * (full + 1) // 2 * LANE + strip * full
    for b in range(RING):
        part[b, last:, :] = jnp.zeros((packed - last, LANE), F32)

    usable = lax.broadcasted_iota(jnp.int32, (LANE, images), 1) < count[0]
    is_one = lax.broadcasted_iota(jnp.int32, (LANE, images), 0) == width % LANE
    pl.semaphore_wait(barrier, 5 * (RING - 1) + 1)

    def pick(t, carry):
        zp = (z + 1 + t) % RING
        load(t).wait()
        group = 32

        def multiply(g, carry):
            at = pl.ds(pl.multiple_of(g * group, group), group)
            chunk = slab[t, at].reshape(group * owned, c_in)
            to = pl.ds(pl.multiple_of(g * group * owned, group * owned), group * owned)
            found = jnp.dot(chunk, onehot[...], preferred_element_type=F32)
            for l in range(cols // LANE):
                picked[l, to, :] = found[:, l * LANE:(l + 1) * LANE]
            return carry

        lax.fori_loop(0, images // group, multiply, 0)
        for j in range(owned):
            yp, k = j // 2, j % 2
            for l in range(cols // LANE):
                height = min(LANE, rows - l * LANE)
                block = picked[l, pl.ds(j, images, stride=owned), :].T[:height]
                if l == width // LANE:
                    block = jnp.where(is_one[:height], 1.0, block)
                block = jnp.where(usable[:height], block, 0.0)
                send[zp, j, l * LANE:l * LANE + height, :] = block.astype(BF16)
            if k == 0:
                to_pos, b, a = zp * RING + y, yp, z
                mine = (c == 0) & (zp == z)
            else:
                to_pos, b, a = z * RING + yp, zp, y
                mine = (c == 1) & (yp == y)
            dst = recv.at[b, :, pl.ds(pl.multiple_of(a * 2 * LANE + c * LANE, LANE), LANE)]

            @pl.when(mine)
            def _():
                pltpu.make_async_copy(send.at[zp, j], dst, recv_sem.at[b, a * 2 + c]).start()

            @pl.when(jnp.logical_not(mine))
            def _():
                pltpu.make_async_remote_copy(
                    src_ref=send.at[zp, j], dst_ref=dst,
                    send_sem=send_sem.at[zp, j], recv_sem=recv_sem.at[b, a * 2 + c],
                    device_id={"img": 2 * x + k, "pos": to_pos}, device_id_type=MESH,
                ).start()

        return carry

    lax.fori_loop(0, RING, pick, 0)

    def rs_copy(b):
        to_pos = (1 - c) * (z * RING + b) + c * (b * RING + y)
        return pltpu.make_async_remote_copy(
            src_ref=part.at[b], dst_ref=rs_recv.at[ring_b],
            send_sem=rs_send.at[b], recv_sem=rs_sem.at[ring_b],
            device_id={"img": img, "pos": to_pos}, device_id_type=MESH,
        )

    def gram(t, carry):
        b = (ring_b + 1 + t) % RING
        for s in range(2 * RING):
            pltpu.make_async_copy(
                send.at[0, 0], recv.at[b, :, s * LANE:(s + 1) * LANE], recv_sem.at[b, s]
            ).wait()
        for i in range(full + (strip > 0)):
            first, height = block_row(i, full, strip)
            wide = min((i + 1) * LANE, rows)
            prod = lax.dot_general(
                recv[b, i * LANE:i * LANE + height, :], recv[b, :wide, :],
                (((1,), (1,)), ((), ())), preferred_element_type=F32,
            )
            for j in range(i + 1):
                w = min(LANE, wide - j * LANE)
                part[b, first + j * height:first + (j + 1) * height, :w] = prod[:, j * LANE:j * LANE + w]

        @pl.when(t < RING - 1)
        def _():
            rs_copy(b).start()

        return carry

    lax.fori_loop(0, RING, gram, 0)

    def rs_wait(d, carry):
        b = (ring_b + d) % RING
        pltpu.make_async_copy(part.at[0], rs_recv.at[b], rs_sem.at[b]).wait()
        part[ring_b] = part[ring_b] + rs_recv[b]
        return carry

    lax.fori_loop(1, RING, rs_wait, 0)

    def rows_of(q):
        return pl.ds(pl.multiple_of(q * piece, 8), piece)

    def ar_copy(d):
        q = (x + d) % RING
        return pltpu.make_async_remote_copy(
            src_ref=part.at[ring_b, rows_of(q)], dst_ref=ar_recv.at[x],
            send_sem=ar_send.at[q], recv_sem=ar_sem.at[x],
            device_id={"img": 2 * q + c, "pos": pos}, device_id_type=MESH,
        )

    def ag_copy(d):
        q = (x + d) % RING
        return pltpu.make_async_remote_copy(
            src_ref=tot.at[c, rows_of(x)], dst_ref=tot.at[c, rows_of(x)],
            send_sem=ag_send.at[q], recv_sem=ag_sem.at[x],
            device_id={"img": 2 * q + c, "pos": pos}, device_id_type=MESH,
        )

    def fw_copy(q):
        return pltpu.make_async_remote_copy(
            src_ref=tot.at[c, rows_of(q)], dst_ref=tot.at[c, rows_of(q)],
            send_sem=fw_send.at[q], recv_sem=fw_sem.at[q],
            device_id={"img": 2 * x + 1 - c, "pos": pos}, device_id_type=MESH,
        )

    for d in (2, 1, 3):
        ar_copy(d).start()
    total = part[ring_b, rows_of(x)]
    for d in (1, 3, 2):
        q = (x + d) % RING
        pltpu.make_async_copy(part.at[0, rows_of(0)], ar_recv.at[q], ar_sem.at[q]).wait()
        total = total + ar_recv[q]
    tot[c, rows_of(x)] = total
    for d in (2, 1, 3):
        ag_copy(d).start()
    fw_copy(x).start()
    for d in (1, 3, 2):
        q = (x + d) % RING
        pltpu.make_async_copy(part.at[0, rows_of(0)], tot.at[c, rows_of(q)], ag_sem.at[q]).wait()
        fw_copy(q).start()
    for q in range(RING):
        pltpu.make_async_copy(part.at[0, rows_of(0)], tot.at[1 - c, rows_of(q)], fw_sem.at[q]).wait()
    write = pltpu.make_async_copy(tot, out, out_sem)
    write.start()

    def sent(t, carry):
        zp = (z + 1 + t) % RING
        for j in range(owned):
            yp, k = j // 2, j % 2
            mine = (c == k) & ((zp == z) if k == 0 else (yp == y))

            @pl.when(jnp.logical_not(mine))
            def _():
                pltpu.make_async_copy(send.at[zp, j], send.at[zp, j], send_sem.at[zp, j]).wait()

        return carry

    lax.fori_loop(0, RING, sent, 0)
    for d in range(1, RING):
        rs_copy((ring_b + d) % RING).wait_send()
        ar_copy(d).wait_send()
        ag_copy(d).wait_send()
    for q in range(RING):
        fw_copy(q).wait_send()
    write.wait()


def finish_kernel(width, tot, centres, covars):
    rows, full, strip, packed = sizes(width)

    def block(p, i, j):
        first, height = block_row(i, full, strip)
        return tot[p, first + j * height:first + (j + 1) * height, :]

    mark = width - full * LANE
    for p in range(tot.shape[0]):
        lin = jnp.concatenate([block(p, full, j)[mark:mark + 1] for j in range(full + 1)], axis=1)
        n = block(p, full, full)[mark:mark + 1, mark:mark + 1]
        centre = lin / n
        centres[p:p + 1, :] = centre[:, :width]
        for i in range(full + 1):
            height = block_row(i, full, strip)[1]
            parts = [block(p, i, j) for j in range(i + 1)]
            for j in range(i + 1, full + 1):
                flip = block(p, j, i).T
                if flip.shape[1] < LANE:
                    flip = jnp.concatenate([flip, jnp.zeros((height, LANE - flip.shape[1]), F32)], axis=1)
                parts.append(flip)
            sums = jnp.concatenate(parts, axis=1)
            own = sums[:, width:width + 1] / n
            spread = (sums - n * (own * centre)) / (n - 1.0)
            row = lax.broadcasted_iota(jnp.int32, sums.shape, 0) + i * LANE
            col = lax.broadcasted_iota(jnp.int32, sums.shape, 1)
            spread = spread + jnp.where(row == col, REG, 0.0)
            keep = min(height, width - i * LANE)
            covars[p, i * LANE:i * LANE + keep, :] = spread[:keep, :width]


def body(features, channel_index, image_counts):
    images, positions, c_in = features.shape
    width = channel_index.shape[0]
    rows, full, strip, packed = sizes(width)
    cols = -(-rows // LANE) * LANE
    owned = positions // RING
    dma = pltpu.SemaphoreType.DMA
    tot = pl.pallas_call(
        functools.partial(gather_kernel, width),
        out_shape=jax.ShapeDtypeStruct((2, packed, LANE), F32),
        in_specs=[
            pl.BlockSpec(memory_space=pl.ANY),
            pl.BlockSpec(memory_space=pltpu.VMEM),
            pl.BlockSpec(memory_space=pltpu.SMEM),
        ],
        out_specs=pl.BlockSpec(memory_space=pl.ANY),
        scratch_shapes=[
            pltpu.VMEM((RING, images, owned, c_in), BF16),
            pltpu.VMEM((c_in, cols), BF16),
            pltpu.VMEM((cols // LANE, images * owned, LANE), F32),
            pltpu.VMEM((RING, owned, rows, images), BF16),
            pltpu.VMEM((RING, rows, 2 * RING * LANE), BF16),
            pltpu.VMEM((RING, packed, LANE), F32),
            pltpu.VMEM((RING, packed, LANE), F32),
            pltpu.VMEM((RING, packed // RING, LANE), F32),
            pltpu.VMEM((2, packed, LANE), F32),
            dma((RING,)),
            dma((RING, owned)),
            dma((RING, 2 * RING)),
            dma((RING,)), dma((RING,)),
            dma((RING,)), dma((RING,)),
            dma((RING,)), dma((RING,)),
            dma((RING,)), dma((RING,)),
            dma,
        ],
        compiler_params=pltpu.CompilerParams(
            collective_id=0, has_side_effects=True, vmem_limit_bytes=56 * 2**20
        ),
        name="pick_and_sum",
    )(features, channel_index.reshape(1, width), image_counts)
    return pl.pallas_call(
        functools.partial(finish_kernel, width),
        out_shape=(
            jax.ShapeDtypeStruct((2, width), F32),
            jax.ShapeDtypeStruct((2, width, width), F32),
        ),
        in_specs=[pl.BlockSpec(memory_space=pltpu.VMEM)],
        out_specs=(pl.BlockSpec(memory_space=pltpu.VMEM), pl.BlockSpec(memory_space=pltpu.VMEM)),
        compiler_params=pltpu.CompilerParams(vmem_limit_bytes=40 * 2**20),
        name="finish",
    )(tot)


def solution(mesh):
    placed = (P(("img", "pos"), None, None), P(), P(("img", "pos")))
    return jax.shard_map(
        body,
        mesh=mesh,
        in_specs=placed,
        out_specs=(P("pos", None), P("pos", None, None)),
        check_vma=False,
    )
```

time: 348 us -> 95.2 us (0.27)
  blocking collectives: 122 us -> 0 us
  Pallas kernels: 0 us -> 87.6 us
  waiting for transfers between devices: 76.9 us -> 0 us
  local copies, waits for them, and re-layouts: 57.5 us -> 5.67 us
  other arithmetic: 45.2 us -> 0 us
  between operations: 14.8 us -> 1.29 us
  loops' own time: 12.4 us -> 0 us
  matrix products: 8.93 us -> 0 us
  starting transfers between devices: 8.68 us -> 0 us
    psum x1 -> x0, blocking collectives: 89.4 us -> none  [body(): group_total = lax.psum(image_counts.astype(jnp.float32)[0], 'pos')]
    pallas_call x0 -> x2, Pallas kernels: none -> 87.6 us  [the longest x1 86 us: body(): pl.pallas_call(functools.partial(gather_kernel, width), out_shape=jax.Sha...]
    all_gather x1 -> x0, waiting for transfers between devices: 76.9 us -> none  [combined_all(): everything = jax.tree.map(lambda part: lax.all_gather(part, axis), value)]
    add x15 -> x0, other arithmetic: 23 us -> none  [the longest x7 17.2 us: combine(): scatter_low + scatter_high]
    unnamed x1 -> x0, blocking collectives: 19.4 us -> none
    unnamed x8 -> x2, local copies, waits for them, and re-layouts: 20.6 us -> 1.4 us
    all_gather x1 -> x0, blocking collectives: 13.3 us -> none  [combined_all(): everything = jax.tree.map(lambda part: lax.all_gather(part, axis), value)]
    gather x2 -> x0, local copies, waits for them, and re-layouts: 13 us -> none  [body(): chosen = jnp.take(masked, channel_index, axis=2)]
  transfers between devices with their start and end apart: 2 -> 0, of which waited for: 1 -> 0; matrix products, arithmetic and copies ran while one was open for 1% -> 0% of each run, Pallas kernels for 0% -> 0%
where the time goes in v1:
time: 95.2 us; the launch traced here: 94.6 us
  Pallas kernels  87.6 us (92%)
  local copies, waits for them, and re-layouts  5.67 us (6%)
  between operations  1.29 us (1%)
    pallas_call x1, Pallas kernels, body(): pl.pallas_call(functools.partial(gather_kernel, width), out_shape=jax.Sha...  86 us
    pallas_call x1, local copies, waits for them, and re-layouts, body(): pl.pallas_call(functools.partial(finish_kernel, width), out_shape=(jax.Sh...  3 us

profile of v1, /device:TPU:1, one launch (start us, length us, event | category | flops | bytes accessed | tf_op | source)
XLA Modules:
  0.0 94.6 jit_solution(18040933896379112163)
XLA Ops:
  1.3 1.3 %reshape.7.chan = s32[1,550]{1,0:T(1,128)} reshape(s32[550]{0:T(1024)} %param.4) | data formatting | bytes 4400 | tf_op jit(solution)/shard_map/reshape | solution.py:311
  2.5 86.0 %pick_and_sum.1.tot = f32[2,1536,128]{2,1,0:T(8,128)} custom-call(bf16[128,32,1536]{2,1,0:T(8,128)(2,1)} %feat.1, s32[1,550]{1,0:T(1,128)} %reshape.7.chan, s32[1]{0:T(128)S(6)} %copy.6.count), custom_call_target="tpu_custom_call" | custom-call | tf_op jit(solution)/shard_map/pick_and_sum/pallas_call | solution.py:279
  88.5 0.0 copy-start
  88.5 1.4 %copy-done = f32[2,1536,128]{2,1,0:T(8,128)S(1)} copy-done((f32[2,1536,128]{2,1,0:T(8,128)S(1)}, f32[2,1536,128]{2,1,0:T(8,128)}, u32[]{:S(2)}) %copy-start) | copy-done | bytes 1572888
  89.9 1.7 %finish.1 = (f32[2,550]{1,0:T(2,128)}, f32[2,550,550]{2,1,0:T(8,128)S(1)}) custom-call(f32[2,1536,128]{2,1,0:T(8,128)S(1)} %copy-done), custom_call_target="tpu_custom_call" | custom-call | tf_op jit(solution)/shard_map/finish/pallas_call | solution.py:312
  91.6 3.0 %copy.5 = f32[2,550,550]{2,0,1:T(2,128)} copy(f32[2,550,550]{2,1,0:T(8,128)S(1)} %get-tuple-element.3) | data formatting | bytes 4840000 | tf_op jit(solution)/shard_map/finish/pallas_call | solution.py:312
Async XLA Ops:
  88.5 1.4 %copy-start = (f32[2,1536,128]{2,1,0:T(8,128)S(1)}, f32[2,1536,128]{2,1,0:T(8,128)}, u32[]{:S(2)}) copy-start(f32[2,1536,128]{2,1,0:T(8,128)} %pick_and_sum.1.tot) | copy-start | bytes 4718596

commit v2 on v1

v2 whole, which is shorter than its diff:
```python
import functools

import jax
import jax.numpy as jnp
from jax import lax
from jax.experimental import pallas as pl
from jax.experimental.pallas import tpu as pltpu
from jax.sharding import PartitionSpec as P

REG = 0.01
MESH = pl.DeviceIdType.MESH
RING = 4
LANE = 128
F32 = jnp.float32
BF16 = jnp.bfloat16


def sizes(width):
    rows = -(-(width + 1) // 16) * 16
    full = (width + 1) // LANE // 2 * 2
    strip = -(-(width + 1 - full * LANE) // 8) * 8
    packed = full * full // 2 * LANE + strip * (full + 1) + full // 2
    return rows, full, strip, -(-packed // 32) * 32


def place(i, j, full, strip):
    if i == full:
        return full * full // 2 * LANE + j * strip
    if i == j:
        return (full * (full - 1) // 2 + i // 2) * LANE
    return (i * (i - 1) // 2 + j) * LANE


def gather_kernel(
    width, feat, chan, count, tot,
    slab, onehot, picked, send, recv, part, x_recv, owned_sum, b_recv,
    load_sem, send_sem, recv_sem, x_send, x_sem, b_send, b_sem, ag_send, ag_sem, fw_send, fw_sem,
):
    rows, full, strip, packed = sizes(width)
    piece = packed // RING
    images, owned = feat.shape[0], feat.shape[1] // RING
    c_in, cols = onehot.shape
    img, pos = lax.axis_index("img"), lax.axis_index("pos")
    x, c = img // 2, img % 2
    z, y = pos // RING, pos % RING
    ring_b = (1 - c) * y + c * z

    barrier = pltpu.get_barrier_semaphore()

    def greet(i, p):
        pl.semaphore_signal(barrier, inc=1, device_id={"img": i, "pos": p}, device_id_type=MESH)

    for d in range(1, RING):
        for k in range(2):
            greet(2 * x + k, (z + d) % RING * RING + y)
            greet(2 * x + k, z * RING + (y + d) % RING)
        greet((x + d) % RING * 2 + c, pos)
    greet(2 * x + 1 - c, pos)

    def load(t):
        zp = (z + 1 + t) % RING
        return pltpu.make_async_copy(
            feat.at[:, pl.ds(zp * owned, owned), :], slab.at[t], load_sem.at[t]
        )

    for t in range(RING):
        load(t).start()

    tail = width // LANE * LANE
    onehot[:, tail:] = jnp.zeros((c_in, cols - tail), BF16)
    step = 256

    def build(i, carry):
        at = pl.ds(pl.multiple_of(i * step, step), step)
        which = lax.broadcasted_iota(jnp.int32, (step, width), 0) + i * step
        onehot[at, :width] = jnp.where(which == chan[...].reshape(1, width), 1.0, 0.0).astype(BF16)
        return carry

    lax.fori_loop(0, c_in // step, build, 0)
    last = place(full, full, full, strip)
    for b in range(RING):
        part[b, last:, :] = jnp.zeros((packed - last, LANE), F32)

    usable = lax.broadcasted_iota(jnp.int32, (LANE, images), 1) < count[0]
    is_one = lax.broadcasted_iota(jnp.int32, (LANE, images), 0) == width % LANE
    pl.semaphore_wait(barrier, 5 * (RING - 1) + 1)

    def exchange(zp, yp, k):
        to_pos = zp * RING + y if k == 0 else z * RING + yp
        b, a = (yp, z) if k == 0 else (zp, y)
        mine = (c == k) & (to_pos == pos)
        src = send.at[zp, 2 * yp + k]
        dst = recv.at[b, :, pl.ds(pl.multiple_of(a * 2 * LANE + c * LANE, LANE), LANE)]

        @pl.when(mine)
        def _():
            pltpu.make_async_copy(src, dst, recv_sem.at[b, a * 2 + c]).start()

        @pl.when(jnp.logical_not(mine))
        def _():
            pltpu.make_async_remote_copy(
                src_ref=src, dst_ref=dst,
                send_sem=send_sem.at[zp, 2 * yp + k], recv_sem=recv_sem.at[b, a * 2 + c],
                device_id={"img": 2 * x + k, "pos": to_pos}, device_id_type=MESH,
            ).start()

    def pick(t, carry):
        zp = (z + 1 + t) % RING
        load(t).wait()
        group = images

        def multiply(g, carry):
            at = pl.ds(pl.multiple_of(g * group, group), group)
            chunk = slab[t, at].reshape(group * owned, c_in)
            to = pl.ds(pl.multiple_of(g * group * owned, group * owned), group * owned)
            found = jnp.dot(chunk, onehot[...], preferred_element_type=F32)
            for l in range(cols // LANE):
                picked[l, to, :] = found[:, l * LANE:(l + 1) * LANE]
            return carry

        lax.fori_loop(0, images // group, multiply, 0)
        for j in range(owned):
            yp, k = j // 2, j % 2
            for l in range(cols // LANE):
                height = min(LANE, rows - l * LANE)
                block = picked[l, pl.ds(j, images, stride=owned), :].T[:height]
                if l == width // LANE:
                    block = jnp.where(is_one[:height], 1.0, block)
                block = jnp.where(usable[:height], block, 0.0)
                send[zp, j, l * LANE:l * LANE + height, :] = block.astype(BF16)
            if k == 0:
                @pl.when(((yp - y + RING) % RING == 1) | ((yp - y + RING) % RING == 2))
                def _():
                    exchange(zp, yp, 0)
            else:
                exchange(zp, yp, 1)

        return carry

    lax.fori_loop(0, RING, pick, 0)

    def rest(t, carry):
        exchange((z + 1 + t % RING) % RING, (y + 3 + t // RING) % RING, 0)
        return carry

    lax.fori_loop(0, 2 * RING, rest, 0)

    def rows_of(q):
        return pl.ds(pl.multiple_of(q * piece, 8), piece)

    def x_copy(b, d):
        q = (x + d) % RING
        return pltpu.make_async_remote_copy(
            src_ref=part.at[b, rows_of(q)], dst_ref=x_recv.at[b, x],
            send_sem=x_send.at[b, q], recv_sem=x_sem.at[b, x],
            device_id={"img": 2 * q + c, "pos": pos}, device_id_type=MESH,
        )

    def b_copy(b):
        to_pos = (1 - c) * (z * RING + b) + c * (b * RING + y)
        return pltpu.make_async_remote_copy(
            src_ref=owned_sum.at[b], dst_ref=b_recv.at[ring_b],
            send_sem=b_send.at[b], recv_sem=b_sem.at[ring_b],
            device_id={"img": img, "pos": to_pos}, device_id_type=MESH,
        )

    row = lax.broadcasted_iota(jnp.int32, (LANE, LANE), 0)
    col = lax.broadcasted_iota(jnp.int32, (LANE, LANE), 1)

    def gram(t):
        b = (ring_b + 1 + t) % RING
        for s in range(2 * RING):
            pltpu.make_async_copy(
                send.at[0, 0], recv.at[b, :, s * LANE:(s + 1) * LANE], recv_sem.at[b, s]
            ).wait()
        for i in range(full + 1):
            height, wide = (LANE, (i + 1) * LANE) if i < full else (strip, full * LANE + strip)
            prod = lax.dot_general(
                recv[b, i * LANE:i * LANE + height, :], recv[b, :wide, :],
                (((1,), (1,)), ((), ())), preferred_element_type=F32,
            )
            for j in range(i + 1):
                first = place(i, j, full, strip)
                w = min(LANE, wide - j * LANE)
                block = prod[:, j * LANE:j * LANE + w]
                if i == j and i % 2 == 1:
                    at = place(full, full, full, strip) + strip + i // 2
                    part[b, at:at + 1, :] = jnp.sum(jnp.where(row == col, block, 0.0), axis=0, keepdims=True)
                    block = jnp.where(row >= col, part[b, first:first + LANE, :], block)
                part[b, first:first + height, :w] = block
        for d in (2, 1, 3):
            x_copy(b, d).start()

    def settle(t):
        b = (ring_b + 1 + t) % RING
        total = part[b, rows_of(x)]
        for d in (1, 3, 2):
            q = (x + d) % RING
            pltpu.make_async_copy(owned_sum.at[0], x_recv.at[b, q], x_sem.at[b, q]).wait()
            total = total + x_recv[b, q]
        owned_sum[b] = total

    gram(0)

    def stage(t, carry):
        gram(t)
        settle(t - 1)
        b_copy((ring_b + t) % RING).start()
        return carry

    lax.fori_loop(1, RING, stage, 0)
    settle(RING - 1)

    def ag_copy(d):
        q = (x + d) % RING
        return pltpu.make_async_remote_copy(
            src_ref=tot.at[c, rows_of(x)], dst_ref=tot.at[c, rows_of(x)],
            send_sem=ag_send.at[q], recv_sem=ag_sem.at[x],
            device_id={"img": 2 * q + c, "pos": pos}, device_id_type=MESH,
        )

    def fw_copy(q):
        return pltpu.make_async_remote_copy(
            src_ref=tot.at[c, rows_of(q)], dst_ref=tot.at[c, rows_of(q)],
            send_sem=fw_send.at[q], recv_sem=fw_sem.at[q],
            device_id={"img": 2 * x + 1 - c, "pos": pos}, device_id_type=MESH,
        )

    total = owned_sum[ring_b]
    for d in (1, 2, 3):
        b = (ring_b + d) % RING
        pltpu.make_async_copy(owned_sum.at[0], b_recv.at[b], b_sem.at[b]).wait()
        total = total + b_recv[b]
    tot[c, rows_of(x)] = total
    for d in (2, 1, 3):
        ag_copy(d).start()
    fw_copy(x).start()
    for d in (1, 3, 2):
        q = (x + d) % RING
        pltpu.make_async_copy(owned_sum.at[0], tot.at[c, rows_of(q)], ag_sem.at[q]).wait()
        fw_copy(q).start()
    for q in range(RING):
        pltpu.make_async_copy(owned_sum.at[0], tot.at[1 - c, rows_of(q)], fw_sem.at[q]).wait()

    def sent(t, carry):
        zp = (z + 1 + t) % RING
        for j in range(owned):
            yp, k = j // 2, j % 2
            mine = (c == k) & ((zp == z) if k == 0 else (yp == y))

            @pl.when(jnp.logical_not(mine))
            def _():
                pltpu.make_async_copy(send.at[zp, j], send.at[zp, j], send_sem.at[zp, j]).wait()

        return carry

    lax.fori_loop(0, RING, sent, 0)
    for d in range(1, RING):
        b_copy((ring_b + d) % RING).wait_send()
        for b in range(RING):
            x_copy(b, d).wait_send()
        ag_copy(d).wait_send()
    for q in range(RING):
        fw_copy(q).wait_send()


def finish_kernel(width, tot, centres, covars):
    rows, full, strip, packed = sizes(width)
    row = lax.broadcasted_iota(jnp.int32, (LANE, LANE), 0)
    col = lax.broadcasted_iota(jnp.int32, (LANE, LANE), 1)
    diagonals = place(full, full, full, strip) + strip

    def block(p, i, j):
        first = place(i, j, full, strip)
        if i == full:
            return tot[p, first:first + strip, :]
        both = tot[p, first:first + LANE, :]
        if i > j:
            return both
        if i % 2 == 0:
            return jnp.where(row >= col, both, both.T)
        at = diagonals + i // 2
        return jnp.where(row == col, tot[p, at:at + 1, :], jnp.where(row < col, both, both.T))

    mark = width - full * LANE
    for p in range(tot.shape[0]):
        lin = jnp.concatenate([block(p, full, j)[mark:mark + 1] for j in range(full + 1)], axis=1)
        n = block(p, full, full)[mark:mark + 1, mark:mark + 1]
        centre = lin / n
        centres[p:p + 1, :] = centre[:, :width]
        for i in range(full + 1):
            height = LANE if i < full else strip
            parts = [block(p, i, j) for j in range(i + 1)]
            for j in range(i + 1, full + 1):
                flip = block(p, j, i).T
                if flip.shape[1] < LANE:
                    flip = jnp.concatenate([flip, jnp.zeros((height, LANE - flip.shape[1]), F32)], axis=1)
                parts.append(flip)
            sums = jnp.concatenate(parts, axis=1)
            own = sums[:, width:width + 1] / n
            spread = (sums - n * (own * centre)) / (n - 1.0)
            at = lax.broadcasted_iota(jnp.int32, sums.shape, 0) + i * LANE
            across = lax.broadcasted_iota(jnp.int32, sums.shape, 1)
            spread = spread + jnp.where(at == across, REG, 0.0)
            keep = min(height, width - i * LANE)
            covars[i * LANE:i * LANE + keep, p, :] = spread[:keep, :width]


def body(features, channel_index, image_counts):
    images, positions, c_in = features.shape
    width = channel_index.shape[0]
    rows, full, strip, packed = sizes(width)
    cols = -(-rows // LANE) * LANE
    owned = positions // RING
    dma = pltpu.SemaphoreType.DMA
    tot = pl.pallas_call(
        functools.partial(gather_kernel, width),
        out_shape=jax.ShapeDtypeStruct((2, packed, LANE), F32),
        in_specs=[
            pl.BlockSpec(memory_space=pl.ANY),
            pl.BlockSpec(memory_space=pltpu.VMEM),
            pl.BlockSpec(memory_space=pltpu.SMEM),
        ],
        out_specs=pl.BlockSpec(memory_space=pltpu.VMEM),
        scratch_shapes=[
            pltpu.VMEM((RING, images, owned, c_in), BF16),
            pltpu.VMEM((c_in, cols), BF16),
            pltpu.VMEM((cols // LANE, images * owned, LANE), F32),
            pltpu.VMEM((RING, owned, rows, images), BF16),
            pltpu.VMEM((RING, rows, 2 * RING * LANE), BF16),
            pltpu.VMEM((RING, packed, LANE), F32),
            pltpu.VMEM((RING, RING, packed // RING, LANE), F32),
            pltpu.VMEM((RING, packed // RING, LANE), F32),
            pltpu.VMEM((RING, packed // RING, LANE), F32),
            dma((RING,)),
            dma((RING, owned)),
            dma((RING, 2 * RING)),
            dma((RING, RING)), dma((RING, RING)),
            dma((RING,)), dma((RING,)),
            dma((RING,)), dma((RING,)),
            dma((RING,)), dma((RING,)),
        ],
        compiler_params=pltpu.CompilerParams(
            collective_id=0, has_side_effects=True, vmem_limit_bytes=56 * 2**20
        ),
        name="pick_and_sum",
    )(features, channel_index, image_counts)
    centres, covars = pl.pallas_call(
        functools.partial(finish_kernel, width),
        out_shape=(
            jax.ShapeDtypeStruct((2, width), F32),
            jax.ShapeDtypeStruct((width, 2, width), F32),
        ),
        in_specs=[pl.BlockSpec(memory_space=pltpu.VMEM)],
        out_specs=(pl.BlockSpec(memory_space=pltpu.VMEM), pl.BlockSpec(memory_space=pltpu.VMEM)),
        compiler_params=pltpu.CompilerParams(vmem_limit_bytes=40 * 2**20),
        name="finish",
    )(tot)
    return centres, jnp.transpose(covars, (1, 0, 2))


def solution(mesh):
    placed = (P(("img", "pos"), None, None), P(), P(("img", "pos")))
    return jax.shard_map(
        body,
        mesh=mesh,
        in_specs=placed,
        out_specs=(P("pos", None), P("pos", None, None)),
        check_vma=False,
    )
```

time: 95.2 us -> 73.7 us (0.77)
  the two profiles are of different devices: /device:TPU:1 before, /device:TPU:49 now
where the time goes in v2:
time: 73.7 us; the launch traced here: 73.5 us
  Pallas kernels  70.9 us (96%)
  local copies, waits for them, and re-layouts  1.3 us (2%)
  between operations  1.29 us (2%)
    pallas_call x1, Pallas kernels, body(): pl.pallas_call(functools.partial(gather_kernel, width), out_shape=jax.Sha...  67.1 us
    pallas_call x1, Pallas kernels, body(): pl.pallas_call(functools.partial(finish_kernel, width), out_shape=(jax.Sh...  3.87 us

profile of v2, /device:TPU:49, one launch (start us, length us, event | category | flops | bytes accessed | tf_op | source)
XLA Modules:
  0.0 73.5 jit_solution(15502144018766551783)
XLA Ops:
  1.3 67.1 %pick_and_sum.1.tot = f32[2,1248,128]{2,1,0:T(8,128)} custom-call(bf16[128,32,1536]{2,1,0:T(8,128)(2,1)} %feat.1, s32[550]{0:T(1024)} %chan.1, s32[1]{0:T(128)S(6)} %copy.5.count), custom_call_target="tpu_custom_call" | custom-call | tf_op jit(solution)/shard_map/pick_and_sum/pallas_call | solution.py:316
  68.4 0.0 copy-start
  68.4 1.3 %copy-done = f32[2,1248,128]{2,1,0:T(8,128)S(1)} copy-done((f32[2,1248,128]{2,1,0:T(8,128)S(1)}, f32[2,1248,128]{2,1,0:T(8,128)}, u32[]{:S(2)}) %copy-start) | copy-done | bytes 1277976
  69.7 3.9 %finish.1 = (f32[2,550]{1,0:T(2,128)}, f32[550,2,550]{2,1,0:T(2,128)}) custom-call(f32[2,1248,128]{2,1,0:T(8,128)S(1)} %copy-done), custom_call_target="tpu_custom_call" | custom-call | tf_op jit(solution)/shard_map/finish/pallas_call | solution.py:348
Async XLA Ops:
  68.4 1.3 %copy-start = (f32[2,1248,128]{2,1,0:T(8,128)S(1)}, f32[2,1248,128]{2,1,0:T(8,128)}, u32[]{:S(2)}) copy-start(f32[2,1248,128]{2,1,0:T(8,128)} %pick_and_sum.1.tot) | copy-start | bytes 3833860

commit v3 on v2

v3 whole, which is shorter than its diff:
```python
import functools

import jax
import jax.numpy as jnp
from jax import lax
from jax.experimental import pallas as pl
from jax.experimental.pallas import tpu as pltpu
from jax.sharding import PartitionSpec as P

REG = 0.01
MESH = pl.DeviceIdType.MESH
RING = 4
LANE = 128
F32 = jnp.float32
BF16 = jnp.bfloat16


HEAD = 3 * LANE


def sizes(width):
    rows = -(-(width + 1) // 16) * 16
    full = (width + 1) // LANE // 2 * 2
    strip = -(-(width + 1 - full * LANE) // 8) * 8
    packed = full * full // 2 * LANE + strip * (full + 1) + full // 2
    return rows, full, strip, -(-packed // 32) * 32


def place(i, j, full, strip):
    if i == full:
        return full * full // 2 * LANE + j * strip
    if i == j:
        i = j = i // 2 * 2 + 1
    return (i * (i - 1) // 2 + i // 2 + j) * LANE


def gather_kernel(
    width, feat, chan, count, tot,
    slab, onehot, picked, send, recv, part, half_recv, quarter_recv, owned_sum, b_recv,
    load_sem, send_sem, recv_sem, half_send, half_sem, quarter_send, quarter_sem, b_send, b_sem,
    near_send, near_sem, far_send, far_sem, fw_send, fw_sem,
):
    rows, full, strip, packed = sizes(width)
    images, owned = feat.shape[0], feat.shape[1] // RING
    c_in, cols = onehot.shape
    img, pos = lax.axis_index("img"), lax.axis_index("pos")
    x, c = img // 2, img % 2
    z, y = pos // RING, pos % RING
    ring_b = (1 - c) * y + c * z
    edge = place(3, 0, full, strip)
    spans = ((0, HEAD), (HEAD, rows - HEAD))
    packs = ((0, edge), (edge, packed - edge))

    other, across = x + 1 - 2 * (x % 2), RING - 1 - x
    first_of = (1 - c) * other + c * across
    second_of = (1 - c) * across + c * other

    def share(core):
        return (1 - core) * ((x + 1) // 2 % 2) + core * (x // 2), (1 - core) * (x // 2) + core * (x % 2)

    mine_h, mine_q = share(c)

    barrier = pltpu.get_barrier_semaphore()

    def greet(i, p):
        pl.semaphore_signal(barrier, inc=1, device_id={"img": i, "pos": p}, device_id_type=MESH)

    for d in range(1, RING):
        for k in range(2):
            greet(2 * x + k, (z + d) % RING * RING + y)
            greet(2 * x + k, z * RING + (y + d) % RING)
    greet(2 * other + c, pos)
    greet(2 * across + c, pos)
    greet(2 * x + 1 - c, pos)

    def turn(t):
        return (1 + 2 * t + t // 2) % RING

    def slab_of(t):
        return (z + turn(t)) % RING

    def load(t):
        return pltpu.make_async_copy(
            feat.at[:, pl.ds(slab_of(t) * owned, owned), :], slab.at[t], load_sem.at[t]
        )

    for t in range(RING):
        load(t).start()

    tail = width // LANE * LANE
    onehot[:, tail:] = jnp.zeros((c_in, cols - tail), BF16)
    step = 256

    def build(i, carry):
        at = pl.ds(pl.multiple_of(i * step, step), step)
        which = lax.broadcasted_iota(jnp.int32, (step, width), 0) + i * step
        onehot[at, :width] = jnp.where(which == chan[...].reshape(1, width), 1.0, 0.0).astype(BF16)
        return carry

    lax.fori_loop(0, c_in // step, build, 0)
    last = place(full, full, full, strip)
    for b in range(RING):
        part[b, last:, :] = jnp.zeros((packed - last, LANE), F32)

    usable = lax.broadcasted_iota(jnp.int32, (LANE, images), 1) < count[0]
    is_one = lax.broadcasted_iota(jnp.int32, (LANE, images), 0) == width % LANE
    pl.semaphore_wait(barrier, 4 * (RING - 1) + 3)

    def exchange(n, zp, yp, k):
        to_pos = zp * RING + y if k == 0 else z * RING + yp
        b, a = (yp, z) if k == 0 else (zp, y)
        mine = (c == k) & (to_pos == pos)
        start, height = spans[n]
        src = send.at[zp, 2 * yp + k, start:start + height]
        dst = recv.at[b, start:start + height, pl.ds(pl.multiple_of(a * 2 * LANE + c * LANE, LANE), LANE)]

        @pl.when(mine)
        def _():
            pltpu.make_async_copy(src, dst, recv_sem.at[n, b, a * 2 + c]).start()

        @pl.when(jnp.logical_not(mine))
        def _():
            pltpu.make_async_remote_copy(
                src_ref=src, dst_ref=dst,
                send_sem=send_sem.at[n, zp, 2 * yp + k], recv_sem=recv_sem.at[n, b, a * 2 + c],
                device_id={"img": 2 * x + k, "pos": to_pos}, device_id_type=MESH,
            ).start()

    def pick(t, carry):
        zp = slab_of(t)
        load(t).wait()
        chunk = slab[t].reshape(images * owned, c_in)
        found = jnp.dot(chunk, onehot[...], preferred_element_type=F32)
        for l in range(cols // LANE):
            picked[l] = found[:, l * LANE:(l + 1) * LANE]
        for j in range(owned):
            yp, k = j // 2, j % 2
            for l in range(cols // LANE):
                height = min(LANE, rows - l * LANE)
                block = picked[l, pl.ds(j, images, stride=owned), :].T[:height]
                if l == width // LANE:
                    block = jnp.where(is_one[:height], 1.0, block)
                block = jnp.where(usable[:height], block, 0.0)
                send[zp, j, l * LANE:l * LANE + height, :] = block.astype(BF16)
            if k == 0:
                @pl.when((yp - y + RING) % 2 == 1)
                def _():
                    exchange(0, zp, yp, 0)
            else:
                exchange(0, zp, yp, 1)
        return carry

    lax.fori_loop(0, RING, pick, 0)

    def rest(t, carry):
        exchange(0, slab_of(t % RING), (y + turn(2 + t // RING)) % RING, 0)
        return carry

    lax.fori_loop(0, 2 * RING, rest, 0)

    def second(t, carry):
        d = turn(t % RING)
        exchange(1, (z + d) % RING, (y + turn(t // RING)) % RING, 0)
        exchange(1, slab_of(t // RING), (y + d) % RING, 1)
        return carry

    lax.fori_loop(0, RING * RING, second, 0)

    def half_rows(n, h):
        start, height = packs[n]
        return pl.ds(pl.multiple_of(start + h * (height // 2), 8), height // 2)

    def quarter_rows(n, h, q):
        start, height = packs[n]
        return pl.ds(pl.multiple_of(start + h * (height // 2) + q * (height // 4), 8), height // 4)

    def kept(n, parts):
        start, height = packs[n]
        return pl.ds(start // parts, height // parts)

    def to(chip, core=None):
        return {"img": 2 * chip + (c if core is None else core), "pos": pos}

    def half_copy(n, b):
        return pltpu.make_async_remote_copy(
            src_ref=part.at[b, half_rows(n, 1 - mine_h)], dst_ref=half_recv.at[b, kept(n, 2)],
            send_sem=half_send.at[n, b], recv_sem=half_sem.at[n, b],
            device_id=to(first_of), device_id_type=MESH,
        )

    def quarter_copy(n, b):
        return pltpu.make_async_remote_copy(
            src_ref=part.at[b, quarter_rows(n, mine_h, 1 - mine_q)], dst_ref=quarter_recv.at[b, kept(n, 4)],
            send_sem=quarter_send.at[n, b], recv_sem=quarter_sem.at[n, b],
            device_id=to(second_of), device_id_type=MESH,
        )

    def b_copy(n, b):
        to_pos = (1 - c) * (z * RING + b) + c * (b * RING + y)
        return pltpu.make_async_remote_copy(
            src_ref=owned_sum.at[b, kept(n, 4)], dst_ref=b_recv.at[ring_b, kept(n, 4)],
            send_sem=b_send.at[n, b], recv_sem=b_sem.at[n, ring_b],
            device_id={"img": img, "pos": to_pos}, device_id_type=MESH,
        )

    def near_copy(n):
        at = quarter_rows(n, mine_h, mine_q)
        return pltpu.make_async_remote_copy(
            src_ref=tot.at[c, at], dst_ref=tot.at[c, at], send_sem=near_send.at[n], recv_sem=near_sem.at[n],
            device_id=to(second_of), device_id_type=MESH,
        )

    def far_copy(n):
        at = half_rows(n, mine_h)
        return pltpu.make_async_remote_copy(
            src_ref=tot.at[c, at], dst_ref=tot.at[c, at], send_sem=far_send.at[n], recv_sem=far_sem.at[n],
            device_id=to(first_of), device_id_type=MESH,
        )

    def fw_copy(n, which, core):
        h, q = share(core)
        at = (quarter_rows(n, h, q), quarter_rows(n, h, 1 - q), half_rows(n, 1 - h))[which]
        return pltpu.make_async_remote_copy(
            src_ref=tot.at[core, at], dst_ref=tot.at[core, at],
            send_sem=fw_send.at[n, which], recv_sem=fw_sem.at[n, which],
            device_id=to(x, 1 - c), device_id_type=MESH,
        )

    row = lax.broadcasted_iota(jnp.int32, (LANE, LANE), 0)
    col = lax.broadcasted_iota(jnp.int32, (LANE, LANE), 1)

    def turn_of(t):
        return (ring_b + turn(t)) % RING

    def gram(n, t):
        b = turn_of(t)
        start, height = spans[n]
        for s in range(2 * RING):
            pltpu.make_async_copy(
                send.at[0, 0, start:start + height],
                recv.at[b, start:start + height, s * LANE:(s + 1) * LANE], recv_sem.at[n, b, s],
            ).wait()
        for i in range(HEAD // LANE * n, HEAD // LANE if n == 0 else full + 1):
            tall, wide = (LANE, (i + 1) * LANE) if i < full else (strip, full * LANE + strip)
            prod = lax.dot_general(
                recv[b, i * LANE:i * LANE + tall, :], recv[b, :wide, :],
                (((1,), (1,)), ((), ())), preferred_element_type=F32,
            )
            for j in range(i + 1):
                first = place(i, j, full, strip)
                w = min(LANE, wide - j * LANE)
                block = prod[:, j * LANE:j * LANE + w]
                if i == j and i % 2 == 1:
                    at = place(full, full, full, strip) + strip + i // 2
                    part[b, at:at + 1, :] = jnp.sum(jnp.where(row == col, block, 0.0), axis=0, keepdims=True)
                    block = jnp.where(row >= col, part[b, first:first + LANE, :], block)
                part[b, first:first + tall, :w] = block
        half_copy(n, b).start()

    def settle_half(n, t):
        b = turn_of(t)
        half_copy(n, b).wait_recv()
        at = half_rows(n, mine_h)
        part[b, at] = part[b, at] + half_recv[b, kept(n, 2)]
        quarter_copy(n, b).start()

    def settle_quarter(n, t):
        b = turn_of(t)
        quarter_copy(n, b).wait_recv()
        owned_sum[b, kept(n, 4)] = part[b, quarter_rows(n, mine_h, mine_q)] + quarter_recv[b, kept(n, 4)]

    def total(n):
        found = owned_sum[ring_b, kept(n, 4)]
        for d in (1, 2, 3):
            b = (ring_b + d) % RING
            pltpu.make_async_copy(owned_sum.at[0, kept(n, 4)], b_recv.at[b, kept(n, 4)], b_sem.at[n, b]).wait()
            found = found + b_recv[b, kept(n, 4)]
        tot[c, quarter_rows(n, mine_h, mine_q)] = found
        near_copy(n).start()
        fw_copy(n, 0, c).start()

    def gather_near(n):
        at = quarter_rows(n, mine_h, 1 - mine_q)
        pltpu.make_async_copy(owned_sum.at[0, kept(n, 4)], tot.at[c, at], near_sem.at[n]).wait()
        far_copy(n).start()
        fw_copy(n, 1, c).start()

    def gather_far(n):
        at = half_rows(n, 1 - mine_h)
        pltpu.make_async_copy(half_recv.at[0, kept(n, 2)], tot.at[c, at], far_sem.at[n]).wait()
        fw_copy(n, 2, c).start()

    def first_chunk(t, carry):
        gram(0, t)

        @pl.when(t >= 1)
        def _():
            settle_half(0, t - 1)

        @pl.when(t >= 2)
        def _():
            settle_quarter(0, t - 2)
            b_copy(0, turn_of(t - 2)).start()

        return carry

    lax.fori_loop(0, RING, first_chunk, 0)

    def second_chunk(t, carry):
        gram(1, t)

        @pl.when(t == 0)
        def _():
            settle_half(0, RING - 1)
            settle_quarter(0, RING - 2)
            b_copy(0, turn_of(RING - 2)).start()

        @pl.when(t == 1)
        def _():
            settle_quarter(0, RING - 1)

        @pl.when(t >= 1)
        def _():
            settle_half(1, t - 1)

        @pl.when(t >= 2)
        def _():
            settle_quarter(1, t - 2)
            b_copy(1, turn_of(t - 2)).start()

        @pl.when(t == 2)
        def _():
            total(0)

        @pl.when(t == 3)
        def _():
            gather_near(0)

        return carry

    lax.fori_loop(0, RING, second_chunk, 0)
    settle_half(1, RING - 1)
    settle_quarter(1, RING - 2)
    b_copy(1, turn_of(RING - 2)).start()
    gather_far(0)
    settle_quarter(1, RING - 1)
    total(1)
    gather_near(1)
    gather_far(1)
    for n in range(2):
        for which in range(3):
            fw_copy(n, which, 1 - c).wait_recv()

    def sent(t, carry):
        zp = slab_of(t)
        for j in range(owned):
            yp, k = j // 2, j % 2
            mine = (c == k) & ((zp == z) if k == 0 else (yp == y))

            @pl.when(jnp.logical_not(mine))
            def _():
                for n in range(2):
                    start, height = spans[n]
                    src = send.at[zp, j, start:start + height]
                    pltpu.make_async_copy(src, src, send_sem.at[n, zp, j]).wait()

        return carry

    lax.fori_loop(0, RING, sent, 0)
    for n in range(2):
        for b in range(RING):
            half_copy(n, b).wait_send()
            quarter_copy(n, b).wait_send()
        for d in range(1, RING):
            b_copy(n, (ring_b + d) % RING).wait_send()
        near_copy(n).wait_send()
        far_copy(n).wait_send()
        for which in range(3):
            fw_copy(n, which, c).wait_send()


def finish_kernel(width, tot, centres, covars):
    rows, full, strip, packed = sizes(width)
    row = lax.broadcasted_iota(jnp.int32, (LANE, LANE), 0)
    col = lax.broadcasted_iota(jnp.int32, (LANE, LANE), 1)
    diagonals = place(full, full, full, strip) + strip

    def block(p, i, j):
        first = place(i, j, full, strip)
        if i == full:
            return tot[p, first:first + strip, :]
        both = tot[p, first:first + LANE, :]
        if i > j:
            return both
        if i % 2 == 0:
            return jnp.where(row >= col, both, both.T)
        at = diagonals + i // 2
        return jnp.where(row == col, tot[p, at:at + 1, :], jnp.where(row < col, both, both.T))

    mark = width - full * LANE
    for p in range(tot.shape[0]):
        lin = jnp.concatenate([block(p, full, j)[mark:mark + 1] for j in range(full + 1)], axis=1)
        n = block(p, full, full)[mark:mark + 1, mark:mark + 1]
        centre = lin / n
        centres[p:p + 1, :] = centre[:, :width]
        for i in range(full + 1):
            height = LANE if i < full else strip
            parts = [block(p, i, j) for j in range(i + 1)]
            for j in range(i + 1, full + 1):
                flip = block(p, j, i).T
                if flip.shape[1] < LANE:
                    flip = jnp.concatenate([flip, jnp.zeros((height, LANE - flip.shape[1]), F32)], axis=1)
                parts.append(flip)
            sums = jnp.concatenate(parts, axis=1)
            own = sums[:, width:width + 1] / n
            spread = (sums - n * (own * centre)) / (n - 1.0)
            at = lax.broadcasted_iota(jnp.int32, sums.shape, 0) + i * LANE
            across = lax.broadcasted_iota(jnp.int32, sums.shape, 1)
            spread = spread + jnp.where(at == across, REG, 0.0)
            keep = min(height, width - i * LANE)
            covars[i * LANE:i * LANE + keep, p, :] = spread[:keep, :width]


def body(features, channel_index, image_counts):
    images, positions, c_in = features.shape
    width = channel_index.shape[0]
    rows, full, strip, packed = sizes(width)
    cols = -(-rows // LANE) * LANE
    owned = positions // RING
    dma = pltpu.SemaphoreType.DMA
    tot = pl.pallas_call(
        functools.partial(gather_kernel, width),
        out_shape=jax.ShapeDtypeStruct((2, packed, LANE), F32),
        in_specs=[
            pl.BlockSpec(memory_space=pl.ANY),
            pl.BlockSpec(memory_space=pltpu.VMEM),
            pl.BlockSpec(memory_space=pltpu.SMEM),
        ],
        out_specs=pl.BlockSpec(memory_space=pltpu.VMEM),
        scratch_shapes=[
            pltpu.VMEM((RING, images, owned, c_in), BF16),
            pltpu.VMEM((c_in, cols), BF16),
            pltpu.VMEM((cols // LANE, images * owned, LANE), F32),
            pltpu.VMEM((RING, owned, rows, images), BF16),
            pltpu.VMEM((RING, rows, 2 * RING * LANE), BF16),
            pltpu.VMEM((RING, packed, LANE), F32),
            pltpu.VMEM((RING, packed // 2, LANE), F32),
            pltpu.VMEM((RING, packed // 4, LANE), F32),
            pltpu.VMEM((RING, packed // 4, LANE), F32),
            pltpu.VMEM((RING, packed // 4, LANE), F32),
            dma((RING,)),
            dma((2, RING, owned)),
            dma((2, RING, 2 * RING)),
            dma((2, RING)), dma((2, RING)),
            dma((2, RING)), dma((2, RING)),
            dma((2, RING)), dma((2, RING)),
            dma((2,)), dma((2,)),
            dma((2,)), dma((2,)),
            dma((2, 3)), dma((2, 3)),
        ],
        compiler_params=pltpu.CompilerParams(
            collective_id=0, has_side_effects=True, vmem_limit_bytes=56 * 2**20
        ),
        name="pick_and_sum",
    )(features, channel_index, image_counts)
    centres, covars = pl.pallas_call(
        functools.partial(finish_kernel, width),
        out_shape=(
            jax.ShapeDtypeStruct((2, width), F32),
            jax.ShapeDtypeStruct((width, 2, width), F32),
        ),
        in_specs=[pl.BlockSpec(memory_space=pltpu.VMEM)],
        out_specs=(pl.BlockSpec(memory_space=pltpu.VMEM), pl.BlockSpec(memory_space=pltpu.VMEM)),
        compiler_params=pltpu.CompilerParams(vmem_limit_bytes=40 * 2**20),
        name="finish",
    )(tot)
    return centres, jnp.transpose(covars, (1, 0, 2))


def solution(mesh):
    placed = (P(("img", "pos"), None, None), P(), P(("img", "pos")))
    return jax.shard_map(
        body,
        mesh=mesh,
        in_specs=placed,
        out_specs=(P("pos", None), P("pos", None, None)),
        check_vma=False,
    )
```

time: 73.7 us -> 79.6 us (1.080)
  the two profiles are of different devices: /device:TPU:49 before, /device:TPU:1 now
where the time goes in v3:
time: 79.6 us; the launch traced here: 79.5 us
  Pallas kernels  76.9 us (97%)
  local copies, waits for them, and re-layouts  1.3 us (2%)
  between operations  1.29 us (2%)
    pallas_call x1, Pallas kernels, body(): pl.pallas_call(functools.partial(gather_kernel, width), out_shape=jax.Sha...  73 us
    pallas_call x1, Pallas kernels, body(): pl.pallas_call(functools.partial(finish_kernel, width), out_shape=(jax.Sh...  3.87 us

profile of v3, /device:TPU:1, one launch (start us, length us, event | category | flops | bytes accessed | tf_op | source)
XLA Modules:
  0.0 79.5 jit_solution(1366878242018144347)
XLA Ops:
  1.3 73.0 %pick_and_sum.1.tot = f32[2,1248,128]{2,1,0:T(8,128)} custom-call(bf16[128,32,1536]{2,1,0:T(8,128)(2,1)} %feat.1, s32[550]{0:T(1024)} %chan.1, s32[1]{0:T(128)S(6)} %copy.5.count), custom_call_target="tpu_custom_call" | custom-call | tf_op jit(solution)/shard_map/pick_and_sum/pallas_call | solution.py:431
  74.3 0.0 copy-start
  74.3 1.3 %copy-done = f32[2,1248,128]{2,1,0:T(8,128)S(1)} copy-done((f32[2,1248,128]{2,1,0:T(8,128)S(1)}, f32[2,1248,128]{2,1,0:T(8,128)}, u32[]{:S(2)}) %copy-start) | copy-done | bytes 1277976
  75.6 3.9 %finish.1 = (f32[2,550]{1,0:T(2,128)}, f32[550,2,550]{2,1,0:T(2,128)}) custom-call(f32[2,1248,128]{2,1,0:T(8,128)S(1)} %copy-done), custom_call_target="tpu_custom_call" | custom-call | tf_op jit(solution)/shard_map/finish/pallas_call | solution.py:466
Async XLA Ops:
  74.3 1.3 %copy-start = (f32[2,1248,128]{2,1,0:T(8,128)S(1)}, f32[2,1248,128]{2,1,0:T(8,128)}, u32[]{:S(2)}) copy-start(f32[2,1248,128]{2,1,0:T(8,128)} %pick_and_sum.1.tot) | copy-start | bytes 3833860

commit v4 on v2

--- a/solution.py
+++ b/solution.py
@@ -57,10 +57,15 @@
         greet((x + d) % RING * 2 + c, pos)
     greet(2 * x + 1 - c, pos)
 
+    def turn(t):
+        return (1 + 2 * t + t // 2) % RING
+
+    def slab_of(t):
+        return (z + turn(t)) % RING
+
     def load(t):
-        zp = (z + 1 + t) % RING
         return pltpu.make_async_copy(
-            feat.at[:, pl.ds(zp * owned, owned), :], slab.at[t], load_sem.at[t]
+            feat.at[:, pl.ds(slab_of(t) * owned, owned), :], slab.at[t], load_sem.at[t]
         )
 
     for t in range(RING):
@@ -104,47 +109,6 @@
                 device_id={"img": 2 * x + k, "pos": to_pos}, device_id_type=MESH,
             ).start()
 
-    def pick(t, carry):
-        zp = (z + 1 + t) % RING
-        load(t).wait()
-        group = images
-
-        def multiply(g, carry):
-            at = pl.ds(pl.multiple_of(g * group, group), group)
-            chunk = slab[t, at].reshape(group * owned, c_in)
-            to = pl.ds(pl.multiple_of(g * group * owned, group * owned), group * owned)
-            found = jnp.dot(chunk, onehot[...], preferred_element_type=F32)
-            for l in range(cols // LANE):
-                picked[l, to, :] = found[:, l * LANE:(l + 1) * LANE]
-            return carry
-
-        lax.fori_loop(0, images // group, multiply, 0)
-        for j in range(owned):
-            yp, k = j // 2, j % 2
-            for l in range(cols // LANE):
-                height = min(LANE, rows - l * LANE)
-                block = picked[l, pl.ds(j, images, stride=owned), :].T[:height]
-                if l == width // LANE:
-                    block = jnp.where(is_one[:height], 1.0, block)
-                block = jnp.where(usable[:height], block, 0.0)
-                send[zp, j, l * LANE:l * LANE + height, :] = block.astype(BF16)
-            if k == 0:
-                @pl.when(((yp - y + RING) % RING == 1) | ((yp - y + RING) % RING == 2))
-                def _():
-                    exchange(zp, yp, 0)
-            else:
-                exchange(zp, yp, 1)
-
-        return carry
-
-    lax.fori_loop(0, RING, pick, 0)
-
-    def rest(t, carry):
-        exchange((z + 1 + t % RING) % RING, (y + 3 + t // RING) % RING, 0)
-        return carry
-
-    lax.fori_loop(0, 2 * RING, rest, 0)
-
     def rows_of(q):
         return pl.ds(pl.multiple_of(q * piece, 8), piece)
 
@@ -168,7 +132,7 @@
     col = lax.broadcasted_iota(jnp.int32, (LANE, LANE), 1)
 
     def gram(t):
-        b = (ring_b + 1 + t) % RING
+        b = (ring_b + turn(t)) % RING
         for s in range(2 * RING):
             pltpu.make_async_copy(
                 send.at[0, 0], recv.at[b, :, s * LANE:(s + 1) * LANE], recv_sem.at[b, s]
@@ -192,7 +156,7 @@
             x_copy(b, d).start()
 
     def settle(t):
-        b = (ring_b + 1 + t) % RING
+        b = (ring_b + turn(t)) % RING
         total = part[b, rows_of(x)]
         for d in (1, 3, 2):
             q = (x + d) % RING
@@ -200,12 +164,56 @@
             total = total + x_recv[b, q]
         owned_sum[b] = total
 
-    gram(0)
+    def pick(t, carry):
+        zp = slab_of(t)
+        load(t).wait()
+        group = images
+
+        def multiply(g, carry):
+            at = pl.ds(pl.multiple_of(g * group, group), group)
+            chunk = slab[t, at].reshape(group * owned, c_in)
+            to = pl.ds(pl.multiple_of(g * group * owned, group * owned), group * owned)
+            found = jnp.dot(chunk, onehot[...], preferred_element_type=F32)
+            for l in range(cols // LANE):
+                picked[l, to, :] = found[:, l * LANE:(l + 1) * LANE]
+            return carry
+
+        lax.fori_loop(0, images // group, multiply, 0)
+        for j in range(owned):
+            for l in range(cols // LANE):
+                height = min(LANE, rows - l * LANE)
+                block = picked[l, pl.ds(j, images, stride=owned), :].T[:height]
+                if l == width // LANE:
+                    block = jnp.where(is_one[:height], 1.0, block)
+                block = jnp.where(usable[:height], block, 0.0)
+                send[zp, j, l * LANE:l * LANE + height, :] = block.astype(BF16)
+        for d in (1, 3, 2, 0):
+            exchange(zp, (y + d) % RING, 1)
+            if d == 1 or d == 3:
+                exchange(zp, (y + d) % RING, 0)
+
+        @pl.when((c == 1) & (t == 2))
+        def _():
+            gram(0)
+
+        return carry
+
+    lax.fori_loop(0, RING, pick, 0)
+
+    def rest(t, carry):
+        exchange(slab_of(t % RING), (y + turn(2 + t // RING)) % RING, 0)
+        return carry
+
+    lax.fori_loop(0, 2 * RING, rest, 0)
+
+    @pl.when(c == 0)
+    def _():
+        gram(0)
 
     def stage(t, carry):
         gram(t)
         settle(t - 1)
-        b_copy((ring_b + t) % RING).start()
+        b_copy((ring_b + turn(t - 1)) % RING).start()
         return carry
 
     lax.fori_loop(1, RING, stage, 0)
@@ -243,7 +251,7 @@
         pltpu.make_async_copy(owned_sum.at[0], tot.at[1 - c, rows_of(q)], fw_sem.at[q]).wait()
 
     def sent(t, carry):
-        zp = (z + 1 + t) % RING
+        zp = slab_of(t)
         for j in range(owned):
             yp, k = j // 2, j % 2
             mine = (c == k) & ((zp == z) if k == 0 else (yp == y))
@@ -315,7 +323,7 @@
     dma = pltpu.SemaphoreType.DMA
     tot = pl.pallas_call(
         functools.partial(gather_kernel, width),
-        out_shape=jax.ShapeDtypeStruct((2, packed, LANE), F32),
+        out_shape=pltpu.VMEM((2, packed, LANE), F32),
         in_specs=[
             pl.BlockSpec(memory_space=pl.ANY),
             pl.BlockSpec(memory_space=pltpu.VMEM),

time: 73.7 us -> 70.5 us (0.957)
  the two profiles are of different devices: /device:TPU:49 before, /device:TPU:1 now
where the time goes in v4:
time: 70.5 us; the launch traced here: 70.4 us
  Pallas kernels  69.1 us (98%)
  between operations  1.28 us (2%)
    pallas_call x1, Pallas kernels, body(): pl.pallas_call(functools.partial(gather_kernel, width), out_shape=pltpu.V...  65.2 us
    pallas_call x1, Pallas kernels, body(): pl.pallas_call(functools.partial(finish_kernel, width), out_shape=(jax.Sh...  3.87 us

profile of v4, /device:TPU:1, one launch (start us, length us, event | category | flops | bytes accessed | tf_op | source)
XLA Modules:
  0.0 70.4 jit_solution(2979381354453977335)
XLA Ops:
  1.3 65.2 %pick_and_sum.1.tot = f32[2,1248,128]{2,1,0:T(8,128)S(1)} custom-call(bf16[128,32,1536]{2,1,0:T(8,128)(2,1)} %feat.1, s32[550]{0:T(1024)} %chan.1, s32[1]{0:T(128)S(6)} %copy.5.count), custom_call_target="tpu_custom_call" | custom-call | tf_op jit(solution)/shard_map/pick_and_sum/pallas_call | solution.py:324
  66.5 3.9 %finish.1 = (f32[2,550]{1,0:T(2,128)}, f32[550,2,550]{2,1,0:T(2,128)}) custom-call(f32[2,1248,128]{2,1,0:T(8,128)S(1)} %pick_and_sum.1.tot), custom_call_target="tpu_custom_call" | custom-call | tf_op jit(solution)/shard_map/finish/pallas_call | solution.py:356

commit v5 on v4

--- a/solution.py
+++ b/solution.py
@@ -45,6 +45,20 @@
     z, y = pos // RING, pos % RING
     ring_b = (1 - c) * y + c * z
 
+    def turn(t):
+        return (1 + 2 * t + t // 2) % RING
+
+    def slab_of(t):
+        return (z + turn(t)) % RING
+
+    def load(t):
+        return pltpu.make_async_copy(
+            feat.at[:, pl.ds(slab_of(t) * owned, owned), :], slab.at[t], load_sem.at[t]
+        )
+
+    for t in range(RING):
+        load(t).start()
+
     barrier = pltpu.get_barrier_semaphore()
 
     def greet(i, p):
@@ -57,20 +71,6 @@
         greet((x + d) % RING * 2 + c, pos)
     greet(2 * x + 1 - c, pos)
 
-    def turn(t):
-        return (1 + 2 * t + t // 2) % RING
-
-    def slab_of(t):
-        return (z + turn(t)) % RING
-
-    def load(t):
-        return pltpu.make_async_copy(
-            feat.at[:, pl.ds(slab_of(t) * owned, owned), :], slab.at[t], load_sem.at[t]
-        )
-
-    for t in range(RING):
-        load(t).start()
-
     tail = width // LANE * LANE
     onehot[:, tail:] = jnp.zeros((c_in, cols - tail), BF16)
     step = 256
@@ -88,7 +88,6 @@
 
     usable = lax.broadcasted_iota(jnp.int32, (LANE, images), 1) < count[0]
     is_one = lax.broadcasted_iota(jnp.int32, (LANE, images), 0) == width % LANE
-    pl.semaphore_wait(barrier, 5 * (RING - 1) + 1)
 
     def exchange(zp, yp, k):
         to_pos = zp * RING + y if k == 0 else z * RING + yp
@@ -131,12 +130,15 @@
     row = lax.broadcasted_iota(jnp.int32, (LANE, LANE), 0)
     col = lax.broadcasted_iota(jnp.int32, (LANE, LANE), 1)
 
-    def gram(t):
+    def arrive(t):
         b = (ring_b + turn(t)) % RING
         for s in range(2 * RING):
             pltpu.make_async_copy(
                 send.at[0, 0], recv.at[b, :, s * LANE:(s + 1) * LANE], recv_sem.at[b, s]
             ).wait()
+
+    def gram(t):
+        b = (ring_b + turn(t)) % RING
         for i in range(full + 1):
             height, wide = (LANE, (i + 1) * LANE) if i < full else (strip, full * LANE + strip)
             prod = lax.dot_general(
@@ -164,7 +166,7 @@
             total = total + x_recv[b, q]
         owned_sum[b] = total
 
-    def pick(t, carry):
+    def pick(t):
         zp = slab_of(t)
         load(t).wait()
         group = images
@@ -187,30 +189,47 @@
                     block = jnp.where(is_one[:height], 1.0, block)
                 block = jnp.where(usable[:height], block, 0.0)
                 send[zp, j, l * LANE:l * LANE + height, :] = block.astype(BF16)
-        for d in (1, 3, 2, 0):
-            exchange(zp, (y + d) % RING, 1)
-            if d == 1 or d == 3:
-                exchange(zp, (y + d) % RING, 0)
-
-        @pl.when((c == 1) & (t == 2))
+
+    def offer(t):
+        zp = slab_of(t)
+        for d in (1, 3):
+            exchange(zp, (y + d) % RING, 0)
+
+        @pl.when(t < 2)
         def _():
-            gram(0)
-
+            for d in (1, 3, 2, 0):
+                exchange(zp, (y + d) % RING, 1)
+
+    def next_slab(t, carry):
+        pick(t)
+        offer(t)
         return carry
 
-    lax.fori_loop(0, RING, pick, 0)
-
-    def rest(t, carry):
-        exchange(slab_of(t % RING), (y + turn(2 + t // RING)) % RING, 0)
-        return carry
-
-    lax.fori_loop(0, 2 * RING, rest, 0)
-
-    @pl.when(c == 0)
-    def _():
-        gram(0)
+    pick(0)
+    pl.semaphore_wait(barrier, 5 * (RING - 1) + 1)
+    offer(0)
+    lax.fori_loop(1, RING, next_slab, 0)
+
+    def later(n):
+        def one(i, carry):
+            d = turn(i)
+            exchange((z + d) % RING, (y + turn(n)) % RING, 0)
+            exchange(slab_of(n), (y + d) % RING, 1)
+            return carry
+
+        lax.fori_loop(0, RING, one, 0)
+
+    arrive(0)
+    later(2)
+    gram(0)
 
     def stage(t, carry):
+        arrive(t)
+
+        @pl.when(t == 1)
+        def _():
+            later(3)
+
         gram(t)
         settle(t - 1)
         b_copy((ring_b + turn(t - 1)) % RING).start()
@@ -272,7 +291,7 @@
         fw_copy(q).wait_send()
 
 
-def finish_kernel(width, tot, centres, covars):
+def finish_kernel(width, tot, centres, covars, made, sem):
     rows, full, strip, packed = sizes(width)
     row = lax.broadcasted_iota(jnp.int32, (LANE, LANE), 0)
     col = lax.broadcasted_iota(jnp.int32, (LANE, LANE), 1)
@@ -291,13 +310,17 @@
         return jnp.where(row == col, tot[p, at:at + 1, :], jnp.where(row < col, both, both.T))
 
     mark = width - full * LANE
+    copies, means = [], []
     for p in range(tot.shape[0]):
         lin = jnp.concatenate([block(p, full, j)[mark:mark + 1] for j in range(full + 1)], axis=1)
         n = block(p, full, full)[mark:mark + 1, mark:mark + 1]
-        centre = lin / n
-        centres[p:p + 1, :] = centre[:, :width]
-        for i in range(full + 1):
-            height = LANE if i < full else strip
+        means.append((n, lin / n))
+        centres[p:p + 1, :] = means[p][1][:, :width]
+    for i in range(full + 1):
+        height = LANE if i < full else strip
+        keep = min(height, width - i * LANE)
+        for p in range(tot.shape[0]):
+            n, centre = means[p]
             parts = [block(p, i, j) for j in range(i + 1)]
             for j in range(i + 1, full + 1):
                 flip = block(p, j, i).T
@@ -310,8 +333,12 @@
             at = lax.broadcasted_iota(jnp.int32, sums.shape, 0) + i * LANE
             across = lax.broadcasted_iota(jnp.int32, sums.shape, 1)
             spread = spread + jnp.where(at == across, REG, 0.0)
-            keep = min(height, width - i * LANE)
-            covars[i * LANE:i * LANE + keep, p, :] = spread[:keep, :width]
+            made[i * LANE:i * LANE + keep, p, :] = spread[:keep, :width]
+        rows_made = slice(i * LANE, i * LANE + keep)
+        copies.append(pltpu.make_async_copy(made.at[rows_made], covars.at[rows_made], sem.at[i]))
+        copies[-1].start()
+    for copy in copies:
+        copy.wait()
 
 
 def body(features, channel_index, image_counts):
@@ -360,7 +387,8 @@
             jax.ShapeDtypeStruct((width, 2, width), F32),
         ),
         in_specs=[pl.BlockSpec(memory_space=pltpu.VMEM)],
-        out_specs=(pl.BlockSpec(memory_space=pltpu.VMEM), pl.BlockSpec(memory_space=pltpu.VMEM)),
+        out_specs=(pl.BlockSpec(memory_space=pltpu.VMEM), pl.BlockSpec(memory_space=pl.ANY)),
+        scratch_shapes=[pltpu.VMEM((width, 2, width), F32), dma((full + 1,))],
         compiler_params=pltpu.CompilerParams(vmem_limit_bytes=40 * 2**20),
         name="finish",
     )(tot)

time: 70.5 us -> 67.4 us (0.956)
  Pallas kernels: 69.1 us -> 65.8 us
    pallas_call x1, Pallas kernels: 65.2 us -> 61.9 us  [body(): pl.pallas_call(functools.partial(gather_kernel, width), out_shape=pltpu.V...]
where the time goes in v5:
time: 67.4 us; the launch traced here: 67.1 us
  Pallas kernels  65.8 us (98%)
  between operations  1.28 us (2%)
    pallas_call x1, Pallas kernels, body(): pl.pallas_call(functools.partial(gather_kernel, width), out_shape=pltpu.V...  61.9 us
    pallas_call x1, Pallas kernels, body(): pl.pallas_call(functools.partial(finish_kernel, width), out_shape=(jax.Sh...  3.85 us

profile of v5, /device:TPU:1, one launch (start us, length us, event | category | flops | bytes accessed | tf_op | source)
XLA Modules:
  0.0 67.1 jit_solution(16974124604165900055)
XLA Ops:
  1.3 61.9 %pick_and_sum.1.tot = f32[2,1248,128]{2,1,0:T(8,128)S(1)} custom-call(bf16[128,32,1536]{2,1,0:T(8,128)(2,1)} %feat.1, s32[550]{0:T(1024)} %chan.1, s32[1]{0:T(128)S(6)} %copy.5.count), custom_call_target="tpu_custom_call" | custom-call | tf_op jit(solution)/shard_map/pick_and_sum/pallas_call | solution.py:351
  63.2 3.9 %finish.1 = (f32[2,550]{1,0:T(2,128)}, f32[550,2,550]{2,1,0:T(2,128)}) custom-call(f32[2,1248,128]{2,1,0:T(8,128)S(1)} %pick_and_sum.1.tot), custom_call_target="tpu_custom_call" | custom-call | tf_op jit(solution)/shard_map/finish/pallas_call | solution.py:383

commit v6 on v5

--- a/solution.py
+++ b/solution.py
@@ -314,13 +314,13 @@
     for p in range(tot.shape[0]):
         lin = jnp.concatenate([block(p, full, j)[mark:mark + 1] for j in range(full + 1)], axis=1)
         n = block(p, full, full)[mark:mark + 1, mark:mark + 1]
-        means.append((n, lin / n))
+        means.append((n, lin / n, 1.0 / (n - 1.0)))
         centres[p:p + 1, :] = means[p][1][:, :width]
     for i in range(full + 1):
         height = LANE if i < full else strip
         keep = min(height, width - i * LANE)
         for p in range(tot.shape[0]):
-            n, centre = means[p]
+            n, centre, scale = means[p]
             parts = [block(p, i, j) for j in range(i + 1)]
             for j in range(i + 1, full + 1):
                 flip = block(p, j, i).T
@@ -329,11 +329,11 @@
                 parts.append(flip)
             sums = jnp.concatenate(parts, axis=1)
             own = sums[:, width:width + 1] / n
-            spread = (sums - n * (own * centre)) / (n - 1.0)
+            spread = (sums - (n * own) * centre) * scale
             at = lax.broadcasted_iota(jnp.int32, sums.shape, 0) + i * LANE
             across = lax.broadcasted_iota(jnp.int32, sums.shape, 1)
             spread = spread + jnp.where(at == across, REG, 0.0)
-            made[i * LANE:i * LANE + keep, p, :] = spread[:keep, :width]
+            made[i * LANE:i * LANE + height, p, :] = spread[:, :width]
         rows_made = slice(i * LANE, i * LANE + keep)
         copies.append(pltpu.make_async_copy(made.at[rows_made], covars.at[rows_made], sem.at[i]))
         copies[-1].start()
@@ -388,7 +388,7 @@
         ),
         in_specs=[pl.BlockSpec(memory_space=pltpu.VMEM)],
         out_specs=(pl.BlockSpec(memory_space=pltpu.VMEM), pl.BlockSpec(memory_space=pl.ANY)),
-        scratch_shapes=[pltpu.VMEM((width, 2, width), F32), dma((full + 1,))],
+        scratch_shapes=[pltpu.VMEM((full * LANE + strip, 2, width), F32), dma((full + 1,))],
         compiler_params=pltpu.CompilerParams(vmem_limit_bytes=40 * 2**20),
         name="finish",
     )(tot)

time: 67.4 us -> 67.3 us (level)
  no operation moved by 1% of the time
where the time goes in v6:
time: 67.3 us; the launch traced here: 67 us
  Pallas kernels  65.7 us (98%)
  between operations  1.28 us (2%)
    pallas_call x1, Pallas kernels, body(): pl.pallas_call(functools.partial(gather_kernel, width), out_shape=pltpu.V...  61.9 us
    pallas_call x1, Pallas kernels, body(): pl.pallas_call(functools.partial(finish_kernel, width), out_shape=(jax.Sh...  3.8 us

profile of v6, /device:TPU:1, one launch (start us, length us, event | category | flops | bytes accessed | tf_op | source)
XLA Modules:
  0.0 67.0 jit_solution(8691749156791856518)
XLA Ops:
  1.3 61.9 %pick_and_sum.1.tot = f32[2,1248,128]{2,1,0:T(8,128)S(1)} custom-call(bf16[128,32,1536]{2,1,0:T(8,128)(2,1)} %feat.1, s32[550]{0:T(1024)} %chan.1, s32[1]{0:T(128)S(6)} %copy.5.count), custom_call_target="tpu_custom_call" | custom-call | tf_op jit(solution)/shard_map/pick_and_sum/pallas_call | solution.py:351
  63.2 3.8 %finish.1 = (f32[2,550]{1,0:T(2,128)}, f32[550,2,550]{2,1,0:T(2,128)}) custom-call(f32[2,1248,128]{2,1,0:T(8,128)S(1)} %pick_and_sum.1.tot), custom_call_target="tpu_custom_call" | custom-call | tf_op jit(solution)/shard_map/finish/pallas_call | solution.py:383
